TPU v7x, 512 devices: a whole 4x4x16 slice. The times are simulated.
512 devices in a mesh: blk: 512 (over y, z, x, core).
Axes of the slice: x: 4, y: 4, z: 16, core: 2. Of those that a mesh axis runs over, the one named last changes fastest.
Arguments:
- tables: float32 [262144, 400], P('blk'), may hold values from -17 to 17
- state: float32 [262144], P('blk'), may hold values from 1e-05 to 0.001
- relations: float32 [2, 400, 400], replicated, may hold values from -0.3125 to 0.3125
- partner: int32 [2, 512], P(None, 'blk'), may hold values from 0 to 511, as said below
- counts: int32 [2, 512], P(None, 'blk'), may hold values from 1 to 512, as said below
- positive: int32 [2, 262144], P(None, 'blk'), may hold values from 0 to 511
- relation_ids: int32 [2, 262144], P(None, 'blk'), may hold values from 0 to 1
Outputs:
- tables_out: float32 [262144, 400], P('blk')
- state_out: float32 [262144], P('blk')
- relations_out: float32 [2, 400, 400], replicated
- losses: float32 [2], replicated
Inputs may be any that keep to these rules, and one draw needn't show every extreme that they name: partner[r, i] = i XOR 2**c_r with one bit number c_r for each round; 512 is a power of two. A block's valid sources in a round are its first counts rows.
All inputs are finite; a program needn't handle non-finite values.
Results may differ from a plain program's by a relative error of at most 0.0078.
Values may be sent and summed in bfloat16 or wider, within the bound.
A program may use at most 64 MiB of HBM per device.

v0:
```python
from functools import partial

import jax
import jax.numpy as jnp
from jax import lax
from jax.sharding import PartitionSpec as P

ROUNDS = 2


learn_rate = 0.3
rel_rate = 0.1


def as_sent(shard):
    return jax.tree.map(lambda a: a.astype(jnp.bfloat16) if a.dtype == jnp.float32 else a, shard)


def partner_2(value, axis, distance):
    mask = 2**distance
    pairs = [(source, source ^ mask) for source in range(lax.axis_size(axis))]
    return lax.ppermute(value, axis, pairs)


def forward(src, dst, rel_ids, pos, count, relb, weight):
    rows = src.shape[0]
    kinds = jnp.arange(relb.shape[0], dtype=jnp.int32)
    choose = (rel_ids[:, None] == kinds[None, :]).astype(jnp.float32)
    query = jnp.zeros((rows, src.shape[1]), jnp.float32)
    for kind in range(relb.shape[0]):
        query = query + choose[:, kind : kind + 1] * jnp.dot(
            src, relb[kind], preferred_element_type=jnp.float32
        )
    query_b = query.astype(jnp.bfloat16)
    scores = lax.dot_general(
        query_b, dst, (((1,), (1,)), ((), ())), preferred_element_type=jnp.float32
    )
    top = jnp.max(scores, axis=1, keepdims=True)
    shifted = jnp.exp(scores - top)
    denom = jnp.sum(shifted, axis=1, keepdims=True)
    columns = jnp.arange(dst.shape[0], dtype=jnp.int32)
    target = (pos[:, None] == columns[None, :]).astype(jnp.float32)
    valid = (jnp.arange(rows, dtype=jnp.int32) < count).astype(jnp.float32)
    per_row = jnp.log(denom[:, 0]) + top[:, 0] - jnp.sum(scores * target, axis=1)
    loss_part = jnp.sum(valid * per_row)
    slope = (weight * valid[:, None] * (shifted / denom - target)).astype(jnp.bfloat16)
    return (loss_part, slope, query_b, choose)


def backward_source(src, dst, slope, choose, relb):
    dquery = jnp.dot(slope, dst, preferred_element_type=jnp.float32).astype(jnp.bfloat16)
    grad_src = jnp.zeros(src.shape, jnp.float32)
    grads = []
    for kind in range(relb.shape[0]):
        part = lax.dot_general(
            dquery, relb[kind], (((1,), (1,)), ((), ())), preferred_element_type=jnp.float32
        )
        grad_src = grad_src + choose[:, kind : kind + 1] * part
        picked = src * choose[:, kind : kind + 1].astype(jnp.bfloat16)
        grads.append(
            lax.dot_general(
                picked, dquery, (((0,), (0,)), ((), ())), preferred_element_type=jnp.float32
            )
        )
    return (grad_src, jnp.stack(grads))


def grad_dest(slope, query_b):
    return lax.dot_general(
        slope, query_b, (((0,), (0,)), ((), ())), preferred_element_type=jnp.float32
    ).astype(jnp.bfloat16)


def route(value, offset, depth, hop):
    branches = [partial(hop, bit=bit) for bit in range(depth)]
    level = jnp.zeros((), jnp.int32)
    for bit in range(1, depth):
        level = level + (offset >> bit > 0).astype(jnp.int32)
    return lax.switch(level, branches, value)


def hop_fetch(value, bit):
    return jax.tree.map(
        lambda part, own: part.astype(own.dtype), partner_2(as_sent(value), "blk", bit), value
    )


def hop_return(value, bit):
    return jax.tree.map(
        lambda part, own: part.astype(own.dtype), partner_2(as_sent(value), "blk", bit), value
    )


def on_device(tables, state, relations, partner, counts, positive, relation_ids):
    self_index = lax.axis_index("blk")
    blocks_all = lax.axis_size("blk")
    depth = blocks_all.bit_length() - 1
    relb = relations.astype(jnp.bfloat16)
    rel_grad = jnp.zeros(relations.shape, jnp.float32)
    loss_parts = []
    totals_list = []
    for rnd in range(ROUNDS):
        totals = lax.psum(counts[rnd, 0].astype(jnp.float32), "blk")
        totals_list.append(totals)
        weight = float(blocks_all) / totals
        offset = jnp.bitwise_xor(partner[rnd, 0], self_index)
        table_b = tables.astype(jnp.bfloat16)
        rid = relation_ids[rnd]
        pos = positive[rnd]
        count = counts[rnd, 0]
        dst = route(table_b, offset, depth, hop_fetch)
        loss_part, slope, query_b, choose = forward(table_b, dst, rid, pos, count, relb, weight)
        grad_src, grads = backward_source(table_b, dst, slope, choose, relb)
        returned = route(grad_dest(slope, query_b), offset, depth, hop_return)
        rel_grad = rel_grad + grads
        loss_parts.append(loss_part)
        grad = grad_src + returned.astype(jnp.float32)
        state = state + jnp.mean(grad * grad, axis=1)
        tables = tables - learn_rate * grad / jnp.sqrt(state)[:, None]
    loss_vec = jnp.stack(loss_parts)
    summed, loss_total = lax.psum((rel_grad, loss_vec), "blk")
    relations_out = relations - rel_rate * summed
    losses = loss_total / jnp.stack(totals_list)
    return (tables, state, relations_out, losses)


def solution(mesh):
    return jax.shard_map(
        on_device,
        mesh=mesh,
        in_specs=(
            P("blk", None),
            P("blk"),
            P(),
            P(None, "blk"),
            P(None, "blk"),
            P(None, "blk"),
            P(None, "blk"),
        ),
        out_specs=(P("blk", None), P("blk"), P(), P()),
        check_vma=False,
    )
```

profile of v0, /device:TPU:1, one launch (start us, length us, event | category | flops | bytes accessed | tf_op | source)
XLA Modules:
  0.0 744.3 jit_solution(14377617215999273336)
XLA Ops:
  14.7 1.5 convert_element_type.288
  16.3 111.0 %psum.28 = f32[]{:T(128)} all-reduce(f32[]{:T(128)S(6)} %convert_element_type.286), channel_id=1, replica_groups=mesh['blk'=512] {'blk'}, use_global_device_ids=true, to_apply=%region_0.0 | all-reduce | flops 1 | bytes 8 | tf_op jit(solution)/shard_map/psum | solution.py:103
  128.6 4.4 conditional.10
  128.6 2.7 collective-permute-start
  131.3 1.6 collective-permute-done
  133.8 1.5 fusion.29
  136.4 1.5 convolution_convert_fusion.3
  137.9 4.2 conditional.11
  138.1 2.3 collective-permute-start.9
  140.4 1.6 collective-permute-done.9
  147.8 3.9 conditional.12
  147.8 2.3 collective-permute-start.18
  150.1 1.6 collective-permute-done.18
  152.9 1.5 fusion.30
  156.0 1.4 pad_maximum_fusion
  157.3 98.9 %all-reduce = (f32[]{:T(128)}, f32[2]{0:T(128)S(1)}) all-reduce(f32[]{:T(128)S(6)} %convert_element_type.304, f32[2]{0:T(128)S(1)} %pad_maximum_fusion), channel_id=1, replica_groups=mesh['blk'=512] {'blk'}, use_global_device_ids=true, to_apply=%region_22.0 | all-reduce | flops 3 | bytes 24 | tf_op jit(solution)/shard_map/psum | solution.py:103
  258.0 1.7 convolution_convert_fusion.1
  261.7 1.5 maximum_add_fusion
  265.2 4.5 conditional.13
  265.4 2.6 collective-permute-start.27
  268.0 1.6 collective-permute-done.27
  271.3 1.9 maximum_divide_fusion
  275.0 459.4 %all-reduce.3.cloned.1.call-done = f32[2,400,400]{2,1,0:T(8,128)} async-done(((f32[2,400,400]{2,1,0:T(8,128)}), f32[2,400,400]{2,1,0:T(8,128)}) %all-reduce.3.cloned.1.call-update) | async-done | bytes 1280016 | tf_op jit(solution)/shard_map/psum | solution.py:121
  734.4 3.0 multiply_subtract_fusion
  (64 shorter events, 24.6 us)
Async XLA Ops:
  7.2 727.3 %all-reduce.3.cloned.1.call-start = ((), (), s32[]{:S(2)}) async-start(), calls=%async_computation | async-start | bytes 3276800 | tf_op jit(solution)/shard_map/psum | solution.py:121
  128.6 4.4 collective-permute-start
  138.1 3.9 collective-permute-start.9
  143.7 0.7 copy-start.9
  143.7 1.4 copy-start
  144.1 0.9 copy-start.2
  147.8 3.9 collective-permute-start.18
  152.2 0.8 copy-start.7
  258.0 2.9 copy-start.5
  263.2 1.0 copy-start.6
  263.2 1.2 copy-start.8
  265.4 4.2 collective-permute-start.27
  270.9 3.0 copy-start.1
  270.9 3.0 copy-start.3
  273.9 460.6 %copy-start.4 = (f32[2,400,400]{2,1,0:T(8,128)S(1)}, f32[2,400,400]{2,1,0:T(8,128)}, u32[]{:S(2)}) copy-start(f32[2,400,400]{2,1,0:T(8,128)} %param.45) | copy-start | bytes 3840004
Sparse Core Ops, SparseCore 0:
  263.4 471.0 all-reduce.2
where the time goes:
time: 757 us; the launch traced here: 744 us
  waiting for transfers between devices  466 us (62%)
  blocking collectives  210 us (28%)
  between operations  18.3 us (2%)
  other arithmetic  16.3 us (2%)
  matrix products  12.2 us (2%)
  local copies, waits for them, and re-layouts  11.4 us (2%)
  starting transfers between devices  9.91 us (1%)
    psum x1, waiting for transfers between devices, on_device(): summed, loss_total = lax.psum((rel_grad, loss_vec), 'blk')  459 us
    psum x2, blocking collectives, on_device(): totals = lax.psum(counts[rnd, 0].astype(jnp.float32), 'blk')  210 us
  transfers between devices with their start and end apart: 5, of which 5 were waited for; matrix products, arithmetic and copies ran while one was open for 1% of the time, Pallas kernels for 0%

commit v1 on v0

v1 whole, which is shorter than its diff:
```python
import functools

import jax
import jax.numpy as jnp
from jax import lax
from jax.experimental import pallas as pl
from jax.experimental.pallas import tpu as pltpu
from jax.sharding import PartitionSpec as P

ROUNDS = 2
LEARN_RATE = 0.3
REL_RATE = 0.1
MESH = pl.DeviceIdType.MESH

NY, NZ, NX = 4, 16, 4
PLANE = NY * NX
LANES = 128
TILES = 80
SHARE = TILES // PLANE
OWNERS = SHARE * 2

VMEM = pl.BlockSpec(memory_space=pltpu.VMEM)
ANY = pl.BlockSpec(memory_space=pl.ANY)


def dot_nn(a, b):
    return lax.dot_general(a, b, (((1,), (0,)), ((), ())), preferred_element_type=jnp.float32)


def dot_nt(a, b):
    return lax.dot_general(a, b, (((1,), (1,)), ((), ())), preferred_element_type=jnp.float32)


def eye(n):
    rows = lax.broadcasted_iota(jnp.int32, (n, n), 0)
    return (rows == lax.broadcasted_iota(jnp.int32, (n, n), 1)).astype(jnp.bfloat16)


def coords():
    me = lax.axis_index("blk")
    core = lax.rem(me, 2)
    x = lax.rem(lax.div(me, 2), NX)
    z = lax.rem(lax.div(me, 2 * NX), NZ)
    y = lax.div(me, 2 * NX * NZ)
    return y, z, x, core


def spots():
    y, z, x, core = coords()
    ys = [lax.rem(y + d, NY) for d in range(NY)]
    zs = [lax.rem(z + d, NZ) for d in range(NZ)]
    xs = [lax.rem(x + d, NX) for d in range(NX)]
    return ys, zs, xs, core


def index_of(y, z, x, core):
    return y * (2 * NX * NZ) + z * (2 * NX) + x * 2 + core


def hops(d, size):
    return min(d, size - d)


PLANE_STEPS = sorted(
    [(dy, dx) for dy in range(NY) for dx in range(NX) if dy or dx],
    key=lambda s: -(hops(s[0], NY) + hops(s[1], NX)))
LINE_STEPS = sorted(range(1, NZ), key=lambda d: -hops(d, NZ))


def greet(peer):
    pl.semaphore_signal(
        pltpu.get_barrier_semaphore(), inc=1, device_id=(peer,), device_id_type=MESH)


def send(src, dst, send_sem, recv_sem, peer):
    return pltpu.make_async_remote_copy(
        src, dst, send_sem, recv_sem, device_id=(peer,), device_id_type=MESH)


def pair_of(bit):
    me = lax.axis_index("blk")
    step = 1 << bit
    return me + step * (1 - 2 * lax.rem(lax.div(me, step), 2))


def own_forms(ebt, rbt, ids, own, query):
    own_t = ebt[...]
    own[...] = dot_nt(eye(own_t.shape[1]), own_t).astype(jnp.bfloat16)
    parts = [dot_nn(rbt[k], own_t) for k in range(rbt.shape[0])]
    query[...] = pick(ids, parts).astype(jnp.bfloat16)


def exchange_first(bit, et, relations, positive, relation_ids, counts,
                   ebt, rb, rbt, meta, ept, metap, tot, own, query,
                   et_v, rel_v, cnt, part, aslot, bslot, loads, sems, asend, arecv, bsend, brecv):
    ys, zs, xs, core = spots()
    partner = pair_of(bit)
    load_e = pltpu.make_async_copy(et, et_v, loads.at[0])
    load_r = pltpu.make_async_copy(relations, rel_v, loads.at[1])
    load_e.start()
    load_r.start()

    near = [index_of(ys[dy], zs[0], xs[dx], core) for dy, dx in PLANE_STEPS]
    near += [index_of(ys[dy], zs[0], xs[dx], 1 - core) for dy, dx in PLANE_STEPS]
    near += [index_of(ys[0], zs[0], xs[0], 1 - core)]
    line = [index_of(ys[0], zs[d], xs[0], core) for d in LINE_STEPS]
    for peer in line + near + [partner]:
        greet(peer)

    meta[0:2, :] = positive[...]
    meta[2:4, :] = relation_ids[...]
    cnt[...] = jnp.zeros(cnt.shape, jnp.float32)
    for rnd in range(ROUNDS):
        one = counts[0:1, rnd : rnd + 1]
        meta[4 + rnd : 5 + rnd, :] = jnp.broadcast_to(one, (1, meta.shape[1]))
        meta[6 + rnd : 7 + rnd, :] = jnp.broadcast_to(one, (1, meta.shape[1]))
        cnt[rnd : rnd + 1, :] = jnp.broadcast_to(one.astype(jnp.float32), (1, LANES))
    load_e.wait()
    ebt[...] = et_v[...].astype(jnp.bfloat16)
    pl.semaphore_wait(pltpu.get_barrier_semaphore(), len(line) + len(near) + 1)

    acopies = [send(cnt, aslot.at[i], asend.at[i], arecv.at[i], peer) for i, peer in enumerate(near)]
    bcopies = [send(part, bslot.at[i], bsend.at[i], brecv.at[i], peer) for i, peer in enumerate(line)]
    small = send(meta, metap, sems.at[2], sems.at[3], partner)
    block = send(ebt, ept, sems.at[0], sems.at[1], partner)
    for c in acopies:
        c.start()
    small.start()
    block.start()

    load_r.wait()
    ident = eye(rb.shape[1])
    for kind in range(rb.shape[0]):
        op = rel_v[kind].astype(jnp.bfloat16)
        rb[kind] = op
        rbt[kind] = dot_nt(ident, op).astype(jnp.bfloat16)

    for c in acopies:
        c.wait()
    part[...] = cnt[...] + jnp.sum(aslot[...], axis=0)
    for c in bcopies:
        c.start()
    own_forms(ebt, rbt, meta[2:3, :], own, query)
    for c in bcopies:
        c.wait()
    tot[...] = part[...] + jnp.sum(bslot[...], axis=0)
    small.wait()
    block.wait()


def exchange_next(bit, ebt, meta, rbt, ept, metap, own, query, sems):
    partner = pair_of(bit)
    greet(partner)
    pl.semaphore_wait(pltpu.get_barrier_semaphore(), 1)
    small = send(meta, metap, sems.at[2], sems.at[3], partner)
    block = send(ebt, ept, sems.at[0], sems.at[1], partner)
    small.start()
    block.start()
    own_forms(ebt, rbt, meta[3:4, :], own, query)
    small.wait()
    block.wait()


def pick(ids, parts):
    out = parts[0]
    for kind in range(1, len(parts)):
        out = jnp.where(ids == kind, parts[kind], out)
    return out


def bucket(dst, query_t, pos, count, weight):
    scores = dot_nn(dst, query_t)
    top = jnp.max(scores, axis=0, keepdims=True)
    shifted = jnp.exp(scores - top)
    denom = jnp.sum(shifted, axis=0, keepdims=True)
    hit = lax.broadcasted_iota(jnp.int32, scores.shape, 0) == pos
    aim = jnp.sum(jnp.where(hit, scores, 0.0), axis=0, keepdims=True)
    valid = lax.broadcasted_iota(jnp.int32, pos.shape, 1) < count
    scale = jnp.where(valid, weight, 0.0)
    slope = scale * (shifted * (1.0 / denom) - jnp.where(hit, 1.0, 0.0))
    rows = jnp.where(valid, jnp.log(denom) + top - aim, 0.0)
    return slope.astype(jnp.bfloat16), rows


def relation_part(kind, rounds, mark, out):
    width = rounds[0][0].shape[0]
    full, tall = width // LANES, width // 16
    main = side = 0.0
    for own_t, dq, ids in rounds:
        picked = jnp.where(ids == kind, own_t, jnp.zeros_like(own_t))
        main = main + dot_nt(picked, dq)
        side = side + dot_nt(dq[full * LANES :, :], picked)
    side = jnp.concatenate([side, jnp.zeros((16, 4 * LANES - width), jnp.float32)], axis=1)
    for j in range(full):
        out[j * tall : (j + 1) * tall] = main[:, j * LANES : (j + 1) * LANES].reshape(tall, 16, LANES)
    for j in range(4):
        out[full * tall + j] = side[:, j * LANES : (j + 1) * LANES]
    out[TILES - 1] = jnp.where(kind == 0, mark, 0.0)


def loss_mark(loss, rnd):
    total = jnp.sum(loss, axis=1, keepdims=True)
    lane = lax.broadcasted_iota(jnp.int32, (16, LANES), 1)
    row = lax.broadcasted_iota(jnp.int32, (16, LANES), 0)
    return jnp.where((lane == rnd) & (row == 0), jnp.broadcast_to(total, (16, LANES)), 0.0)


def gradients(rnd, blocks, ept, own, query, meta, metap, tot, rb, rbt, then):
    kinds = rb.shape[0]
    far_t = ept[...]
    far = dot_nt(eye(far_t.shape[1]), far_t).astype(jnp.bfloat16)
    weight = blocks / tot[rnd : rnd + 1, 0:1]
    pos, ids, count = meta[rnd : rnd + 1, :], meta[2 + rnd : 3 + rnd, :], meta[4 + rnd : 5 + rnd, :]
    pos_p, ids_p = metap[rnd : rnd + 1, :], metap[2 + rnd : 3 + rnd, :]
    count_p = metap[4 + rnd : 5 + rnd, :]

    slope, loss = bucket(far, query[...], pos, count, weight)
    dq = dot_nn(far_t, slope).astype(jnp.bfloat16)
    then(ids, dq, loss_mark(loss, rnd))
    query_p = pick(ids_p, [dot_nn(rbt[k], far_t) for k in range(kinds)]).astype(jnp.bfloat16)
    slope_p, _ = bucket(own[...], query_p, pos_p, count_p, weight)
    grad = pick(ids, [dot_nn(rb[k], dq) for k in range(kinds)])
    return grad + dot_nt(query_p, slope_p).astype(jnp.bfloat16).astype(jnp.float32)


def adagrad(et, state, grad):
    acc = state + jnp.mean(grad * grad, axis=0, keepdims=True)
    return acc, et - LEARN_RATE * grad / jnp.sqrt(acc)


def round_kernel(blocks, et, ept, own, query, meta, metap, tot, state, rb, rbt,
                 et_out, ebt_out, state_out, dq_out, mark_out, et_v, loads):
    load_e = pltpu.make_async_copy(et, et_v, loads.at[0])
    load_e.start()

    def keep(ids, dq, mark):
        dq_out[...] = dq
        mark_out[...] = mark

    grad = gradients(0, blocks, ept, own, query, meta, metap, tot, rb, rbt, keep)
    load_e.wait()
    acc, fresh = adagrad(et_v[...], state[...], grad)
    state_out[...] = acc
    et_out[...] = fresh
    ebt_out[...] = fresh.astype(jnp.bfloat16)


def last_kernel(blocks, et, ebt, ept, own, query, meta, metap, tot, state, rb, rbt, ebt_a, dq_a, mark_a, relations,
                et_out, state_out, rel_out, loss_out,
                rel_v, grad_v, csend, crecv, acc, xsend, xslot, zpart, zslot, zres, fin, sib,
                loads, s_core, s_xs, s_xr, s_zs, s_zr, s_gs, s_gr, s_as, s_ar, s_bs, s_br):
    ys, zs, xs, core = spots()
    back_y = [lax.rem(ys[0] + NY - d, NY) for d in range(NY)]
    back_x = [lax.rem(xs[0] + NX - d, NX) for d in range(NX)]
    z = zs[0]
    plane = ys[0] * NX + xs[0]
    other = 1 - core
    twin = index_of(ys[0], z, xs[0], other)
    near = [index_of(ys[dy], z, xs[dx], core) for dy, dx in PLANE_STEPS]
    near_plane = [ys[dy] * NX + xs[dx] for dy, dx in PLANE_STEPS]
    from_plane = [back_y[dy] * NX + back_x[dx] for dy, dx in PLANE_STEPS]
    line = [index_of(ys[0], zs[d], xs[0], core) for d in LINE_STEPS]
    line_z = [zs[d] for d in LINE_STEPS]
    places = range(PLANE - 1)
    steps = range(NZ - 1)

    for peer in line + near + [twin]:
        greet(peer)
    load_r = pltpu.make_async_copy(relations, rel_v, loads.at[0])
    load_r.start()

    kept = []

    def relation_first(ids, dq, mark):
        kept.append([(ebt_a[...], dq_a[...], meta[2:3, :]), (ebt[...], dq, ids)])
        kept.append(mark + mark_a[...])
        relation_part(other, *kept, csend)

    grad_v[...] = gradients(1, blocks, ept, own, query, meta, metap, tot, rb, rbt, relation_first)
    pl.semaphore_wait(pltpu.get_barrier_semaphore(), len(line) + len(near) + 1)

    swap = send(csend, crecv, s_core.at[0], s_core.at[1], twin)
    swap.start()
    relation_part(core, *kept, acc)
    swap.wait()
    both = acc[...] + crecv[...]
    acc[...] = both
    xsend[...] = both.astype(jnp.bfloat16).reshape(PLANE, SHARE, 16, LANES)

    xcopies = [send(xsend.at[near_plane[i]], xslot.at[i], s_xs.at[i], s_xr.at[i], near[i]) for i in places]
    for c in xcopies:
        c.start()
    acc_s, fresh = adagrad(et[...], state[...], grad_v[...])
    state_out[...] = acc_s
    et_out[...] = fresh
    for c in xcopies:
        c.wait()
    part = acc[pl.ds(plane * SHARE, SHARE)]
    for i in places:
        part = part + xslot[i].astype(jnp.float32)
    zpart[...] = part.reshape(OWNERS, 8, LANES)

    def zcopy(i, piece):
        return send(zpart.at[piece], zslot.at[i], s_zs.at[i], s_zr.at[i], line[i])

    def gcopy(i, owner):
        return send(zres.at[owner], zres.at[owner], s_gs.at[i], s_gr.at[owner], line[i])

    for i in steps:
        @pl.when(line_z[i] < OWNERS)
        def _():
            zcopy(i, line_z[i]).start()

    @pl.when(z < OWNERS)
    def _():
        for i in steps:
            zcopy(i, 0).wait_recv()
        total = zpart[z]
        for i in steps:
            total = total + zslot[i]
        zres[z] = total
        for i in steps:
            gcopy(i, z).start()

    for i in steps:
        @pl.when(line_z[i] < OWNERS)
        def _():
            zcopy(i, line_z[i]).wait_send()

    for o in range(OWNERS):
        @pl.when(z != o)
        def _():
            gcopy(0, o).wait_recv()

    whole = zres[...].reshape(SHARE, 16, LANES)
    tail = whole[SHARE - 1]
    rest = tail[0:8] - tail[0:8].astype(jnp.bfloat16).astype(jnp.float32)
    tail = jnp.concatenate([tail[0:8], jnp.where(plane == PLANE - 1, rest, tail[8:16])], axis=0)
    fin[plane] = whole.astype(jnp.bfloat16)
    fin[plane, SHARE - 1] = tail.astype(jnp.bfloat16)

    def ncopy(i, piece):
        return send(fin.at[piece], fin.at[piece], s_as.at[i], s_ar.at[i], near[i])

    def tcopy(piece, slot):
        return send(fin.at[piece], sib.at[piece], s_bs.at[slot], s_br.at[slot], twin)

    for i in places:
        ncopy(i, plane).start()
    tcopy(plane, PLANE - 1).start()

    @pl.when(z < OWNERS)
    def _():
        for i in steps:
            gcopy(i, z).wait_send()

    load_r.wait()
    for i in reversed(places):
        ncopy(i, from_plane[i]).wait_recv()
        tcopy(from_plane[i], i).start()

    width = rel_v.shape[1]
    full = width // LANES
    tall = width // 16
    edge = full * LANES

    def finish(kind, ref):
        summed = ref[...].reshape(TILES, 16, LANES).astype(jnp.float32)
        for j in range(full):
            piece = summed[j * tall : (j + 1) * tall].reshape(width, LANES)
            span = slice(j * LANES, (j + 1) * LANES)
            rel_out[kind, :, span] = rel_v[kind, :, span] - REL_RATE * piece
        side = jnp.concatenate([summed[full * tall + j] for j in range(4)], axis=1)
        rel_out[kind, :, edge:] = rel_v[kind, :, edge:] - REL_RATE * side.T[:width, :]

    finish(core, fin)
    for i in reversed(places):
        tcopy(from_plane[i], i).wait()
    tcopy(plane, PLANE - 1).wait()
    for i in places:
        ncopy(i, plane).wait_send()
    finish(other, sib)

    def losses(ref):
        tile = ref[PLANE - 1, SHARE - 1].astype(jnp.float32)
        sums = tile[0:1] + tile[8:9]
        for rnd in range(ROUNDS):
            span = slice(rnd, rnd + 1)
            loss_out[:, span] = sums[:, span] / tot[span, 0:1]

    @pl.when(core == 0)
    def _():
        losses(fin)

    @pl.when(core == 1)
    def _():
        losses(sib)


def on_device(tables, state, relations, partner, counts, positive, relation_ids):
    rows, width = tables.shape
    blocks = lax.axis_size("blk")
    depth = blocks.bit_length() - 1
    me = lax.axis_index("blk")
    f32, bf16, i32 = jnp.float32, jnp.bfloat16, jnp.int32
    shape = jax.ShapeDtypeStruct
    DMA = pltpu.SemaphoreType.DMA
    block_f, block_b, flat_b = shape((width, rows), f32), shape((width, rows), bf16), shape((rows, width), bf16)
    ops_b, small_i, tile_f = shape(relations.shape, bf16), shape((8, rows), i32), shape((8, LANES), f32)
    accum_f, mark_f = shape((1, rows), f32), shape((16, LANES), f32)
    partial = functools.partial

    offset = jnp.bitwise_xor(partner[:, 0], me)
    level = jnp.zeros((ROUNDS,), i32)
    for bit in range(1, depth):
        level = level + (offset >> bit > 0).astype(i32)

    def first(bit, *args):
        return pl.pallas_call(
            partial(exchange_first, bit),
            out_shape=(block_b, ops_b, ops_b, small_i, block_b, small_i, tile_f, flat_b, block_b),
            in_specs=[ANY, ANY, VMEM, VMEM, VMEM],
            out_specs=(VMEM,) * 9,
            scratch_shapes=[
                pltpu.VMEM((width, rows), f32),
                pltpu.VMEM(relations.shape, f32),
                pltpu.VMEM((8, LANES), f32),
                pltpu.VMEM((8, LANES), f32),
                pltpu.VMEM((2 * PLANE - 1, 8, LANES), f32),
                pltpu.VMEM((NZ - 1, 8, LANES), f32),
                DMA((2,)),
                DMA((4,)),
                DMA((2 * PLANE - 1,)), DMA((2 * PLANE - 1,)),
                DMA((NZ - 1,)), DMA((NZ - 1,)),
            ],
            compiler_params=pltpu.CompilerParams(collective_id=bit, has_side_effects=True),
            name="swap_a",
        )(*args)

    def following(bit, *args):
        return pl.pallas_call(
            partial(exchange_next, bit),
            out_shape=(block_b, small_i, flat_b, block_b),
            in_specs=[VMEM] * 3,
            out_specs=(VMEM,) * 4,
            scratch_shapes=[DMA((4,))],
            compiler_params=pltpu.CompilerParams(collective_id=depth + bit, has_side_effects=True),
            name="swap_b",
        )(*args)

    et = tables.T
    accum = state.reshape(1, rows)
    ebt, rb, rbt, meta, ept, metap, tot, own, query = lax.switch(
        level[0], [partial(first, bit) for bit in range(depth)],
        et, relations, positive, relation_ids, counts.T)
    et, ebt2, accum, dq, mark = pl.pallas_call(
        partial(round_kernel, float(blocks)),
        out_shape=(block_f, block_b, accum_f, block_b, mark_f),
        in_specs=[ANY] + [VMEM] * 9,
        out_specs=(VMEM,) * 5,
        scratch_shapes=[pltpu.VMEM((width, rows), f32), DMA((1,))],
        name="round_a",
    )(et, ept, own, query, meta, metap, tot, accum, rb, rbt)

    ept, metap, own, query = lax.switch(
        level[1], [partial(following, bit) for bit in range(depth)],
        ebt2, meta, rbt)
    et, accum, relations_out, losses = pl.pallas_call(
        partial(last_kernel, float(blocks)),
        out_shape=(block_f, accum_f, shape(relations.shape, f32), shape((1, ROUNDS), f32)),
        in_specs=[VMEM] * 14 + [ANY],
        out_specs=(VMEM,) * 4,
        scratch_shapes=[
            pltpu.VMEM(relations.shape, f32),
            pltpu.VMEM((width, rows), f32),
            pltpu.VMEM((TILES, 16, LANES), f32),
            pltpu.VMEM((TILES, 16, LANES), f32),
            pltpu.VMEM((TILES, 16, LANES), f32),
            pltpu.VMEM((PLANE, SHARE, 16, LANES), bf16),
            pltpu.VMEM((PLANE - 1, SHARE, 16, LANES), bf16),
            pltpu.VMEM((OWNERS, 8, LANES), f32),
            pltpu.VMEM((NZ - 1, 8, LANES), f32),
            pltpu.VMEM((OWNERS, 8, LANES), f32),
            pltpu.VMEM((PLANE, SHARE, 16, LANES), bf16),
            pltpu.VMEM((PLANE, SHARE, 16, LANES), bf16),
            DMA((1,)),
            DMA((2,)),
            DMA((PLANE - 1,)), DMA((PLANE - 1,)),
            DMA((NZ - 1,)), DMA((NZ - 1,)),
            DMA((NZ - 1,)), DMA((OWNERS,)),
            DMA((PLANE - 1,)), DMA((PLANE - 1,)),
            DMA((PLANE,)), DMA((PLANE,)),
        ],
        compiler_params=pltpu.CompilerParams(collective_id=2 * depth, has_side_effects=True),
        name="last",
    )(et, ebt2, ept, own, query, meta, metap, tot, accum, rb, rbt, ebt, dq, mark, relations)
    return (et.T, accum.reshape(rows), relations_out, losses.reshape(ROUNDS))


def solution(mesh):
    return jax.shard_map(
        on_device,
        mesh=mesh,
        in_specs=(
            P("blk", None),
            P("blk"),
            P(),
            P(None, "blk"),
            P(None, "blk"),
            P(None, "blk"),
            P(None, "blk"),
        ),
        out_specs=(P("blk", None), P("blk"), P(), P()),
        check_vma=False,
    )
```

time: 757 us -> 132 us (0.17); the launches traced: 744 us -> 131 us
  waiting for transfers between devices: 466 us -> 0 us
  blocking collectives: 210 us -> 0 us
  Pallas kernels: 0 us -> 123 us
  between operations: 18.3 us -> 2.02 us
  other arithmetic: 16.3 us -> 0.67 us
  matrix products: 12.2 us -> 0 us
  starting transfers between devices: 9.91 us -> 0 us
    psum x1 -> x0, waiting for transfers between devices: 459 us -> none  [on_device(): summed, loss_total = lax.psum((rel_grad, loss_vec), 'blk')]
    psum x2 -> x0, blocking collectives: 210 us -> none  [on_device(): totals = lax.psum(counts[rnd, 0].astype(jnp.float32), 'blk')]
    pallas_call x0 -> x4, Pallas kernels: none -> 123 us  [the longest x1 43.8 us: following(): pl.pallas_call(partial(exchange_next, bit), out_shape=(block_b, small_i,...]
    dot_general x18 -> x0, matrix products: 12.2 us -> none  [the longest x2 3.12 us: backward_source(): jnp.dot(slope, dst, preferred_element_type=jnp.float32).astype(jnp.bfloat16)]
    ppermute x4 -> x0, starting transfers between devices: 9.87 us -> none  [partner_2(): return lax.ppermute(value, axis, pairs)]
  transfers between devices with their start and end apart: 5 -> 0, of which waited for: 5 -> 0; matrix products, arithmetic and copies ran while one was open for 1% -> 0% of each run, Pallas kernels for 0% -> 0%
where the time goes in v1:
time: 132 us; the launch traced here: 131 us
  Pallas kernels  123 us (93%)
  local copies, waits for them, and re-layouts  5.07 us (4%)
  between operations  2.02 us (2%)
    pallas_call x1, Pallas kernels, following(): pl.pallas_call(partial(exchange_next, bit), out_shape=(block_b, small_i,...  43.8 us
    pallas_call x1, Pallas kernels, on_device(): pl.pallas_call(partial(last_kernel, float(blocks)), out_shape=(block_f, a...  43.2 us
    pallas_call x1, Pallas kernels, first(): pl.pallas_call(partial(exchange_first, bit), out_shape=(block_b, ops_b, o...  30.2 us
    pallas_call x1, Pallas kernels, on_device(): pl.pallas_call(partial(round_kernel, float(blocks)), out_shape=(block_f,...  5.72 us
    unnamed x14, local copies, waits for them, and re-layouts  4.49 us

profile of v1, /device:TPU:1, one launch (start us, length us, event | category | flops | bytes accessed | tf_op | source)
XLA Modules:
  0.0 131.4 jit_solution(13445760032365163014)
XLA Ops:
  0.6 0.7 fusion.6
  1.3 0.6 fusion.7
  3.2 30.6 %conditional.2 = ((bf16[400,512]{1,0:T(8,128)(2,1)}, bf16[2,400,400]{2,1,0:T(8,128)(2,1)S(1)}, bf16[2,400,400]{2,1,0:T(8,128)(2,1)S(1)}, s32[8,512]{1,0:T(8,128)...) conditional(s32[]{:T(128)} %bitcast.1, (f32[400,512]{1,0:T(8,128)}, ...), branch_computations={%region_0.0_spmd, %region_1.0_spmd, %region_2.0_spmd, %region_3.0_... | conditional | bytes 8 | solution.py:453
  3.4 30.2 %swap_a.16 = (bf16[400,512]{1,0:T(8,128)(2,1)}, bf16[2,400,400]{2,1,0:T(8,128)(2,1)S(1)}, bf16[2,400,400]{2,1,0:T(8,128)(2,1)S(1)}, s32[8,512]{1,0:T(8,128)S(1)}...) custom-call(f32[400,512]{1,0:T(8,128)} %get-tuple-element.179.et, ...), custom_call_target="tpu_custom_call" | custom-call | tf_op jit(solution)/shard_map/cond/branch_7_fun/swap_a/pallas_call | solution.py:419
  33.8 0.0 copy-start.1
  33.8 5.7 %round_a.1 = (f32[400,512]{1,0:T(8,128)}, bf16[400,512]{1,0:T(8,128)(2,1)S(1)}, f32[1,512]{1,0:T(1,128)}, bf16[400,512]{1,0:T(8,128)(2,1)}, f32[16,128]{1,0:T(8,128)}) custom-call(f32[400,512]{1,0:T(8,128)} %bitcast.17, bf16[400,512]{1,0:T(8,128)(2,1)S(1)} %get-tuple-element.242.ept, bf16[512,400]{1,0:T(8,128)(2,1)S(1)} %get-tuple-element.243.own, ...), custom_call_target="tpu_custom_call" | custom-call | tf_op jit(solution)/shard_map/round_a/pallas_call | solution.py:456
  39.6 0.0 copy-done.1
  39.6 0.0 copy-start
  39.6 44.1 %conditional.3 = ((bf16[400,512]{1,0:T(8,128)(2,1)}, s32[8,512]{1,0:T(8,128)S(1)}, bf16[512,400]{1,0:T(8,128)(2,1)S(1)}, bf16[400,512]{1,0:T(8,128)(2,1)})) conditional(s32[]{:T(128)} %bitcast.4, (bf16[400,512]{1,0:T(8,128)(2,1)S(1)}, s32[8,512]{1,0:T(8,128)S(1)}, bf16[2,400,400]{2,1,0:T(8,128)(2,1)S(1)}) %tuple.63, ...), branch_computations={%region_9.0_spmd, %region_10.0_spmd, %region_11.0_spmd, %region_12... | conditional | bytes 8 | solution.py:465
  39.6 43.8 %swap_b.14 = (bf16[400,512]{1,0:T(8,128)(2,1)}, s32[8,512]{1,0:T(8,128)S(1)}, bf16[512,400]{1,0:T(8,128)(2,1)S(1)}, bf16[400,512]{1,0:T(8,128)(2,1)}) custom-call(bf16[400,512]{1,0:T(8,128)(2,1)S(1)} %get-tuple-element.204.ebt, s32[8,512]{1,0:T(8,128)S(1)} %get-tuple-element.205.meta, bf16[2,400,400]{2,1,0:T(8,128)(2,1)S(1)} %get-tuple-element.206.rbt), custom_call_target="tpu_custom_call" | custom-call | tf_op jit(solution)/shard_map/cond/branch_5_fun/swap_b/pallas_call | solution.py:441
  83.7 0.0 copy-done
  83.7 43.2 %last.1 = (f32[400,512]{1,0:T(8,128)}, f32[1,512]{1,0:T(1,128)}, f32[2,400,400]{2,1,0:T(8,128)}, f32[1,2]{1,0:T(1,128)}) custom-call(f32[400,512]{1,0:T(8,128)} %get-tuple-element.250.et, bf16[400,512]{1,0:T(8,128)(2,1)S(1)} %get-tuple-element.251.ebt, bf16[400,512]{1,0:T(8,128)(2,1)} %get-tuple-element.252.ept, ...), custom_call_target="tpu_custom_call" | custom-call | tf_op jit(solution)/shard_map/last/pallas_call | solution.py:468
  126.9 0.0 copy-start.3
  126.9 0.0 copy-start.2
  126.9 2.2 %copy.132 = f32[512,400]{0,1:T(8,128)} copy(f32[512,400]{0,1:T(8,128)} %bitcast.18) | data formatting | bytes 1638400
  129.1 0.0 copy-done.3
  129.1 0.6 copy.133
  129.7 0.0 copy-done.2
  129.7 0.0 copy-start.4
  129.7 1.2 copy.134
  130.9 0.0 copy-done.4
  130.9 0.5 copy.135
Async XLA Ops:
  33.8 5.7 %copy-start.1 = (bf16[2,400,400]{2,1,0:T(8,128)(2,1)}, bf16[2,400,400]{2,1,0:T(8,128)(2,1)S(1)}, u32[]{:S(2)}) copy-start(bf16[2,400,400]{2,1,0:T(8,128)(2,1)S(1)} %get-tuple-element.248.rb) | copy-start | bytes 1920004
  39.6 44.1 %copy-start = (f32[2,400,400]{2,1,0:T(8,128)S(1)}, f32[2,400,400]{2,1,0:T(8,128)}, u32[]{:S(2)}) copy-start(f32[2,400,400]{2,1,0:T(8,128)} %relations.1) | copy-start | bytes 3840004
  126.9 2.2 %copy-start.3 = (f32[1,512]{1,0:T(1,128)S(1)}, f32[1,512]{1,0:T(1,128)}, u32[]{:S(2)}) copy-start(f32[1,512]{1,0:T(1,128)} %get-tuple-element.261) | copy-start | bytes 6148
  126.9 2.8 %copy-start.2 = (f32[2,400,400]{2,1,0:T(8,128)S(1)}, f32[2,400,400]{2,1,0:T(8,128)}, u32[]{:S(2)}) copy-start(f32[2,400,400]{2,1,0:T(8,128)} %get-tuple-element.389) | copy-start | bytes 3840004
  129.7 1.2 copy-start.4
